TPU v7x, 32 devices: a whole 2x2x4 slice. The times are simulated.
32 devices in a mesh: seq: 8 (over y, x, core), batch: 4 (over z).
Axes of the slice: x: 2, y: 2, z: 4, core: 2. Of those that a mesh axis runs over, the one named last changes fastest.
Arguments:
- stream_in: bfloat16 [16, 2048, 768], P('batch', 'seq'), may hold values from -6 to 6
- lengths: int32 [16], P('batch'), may hold values from 64 to 2048, as said below
- token_mask: int32 [16, 2048], P('batch', 'seq'), may hold values from 0 to 1, as said below
- norm1_gain: bfloat16 [768], replicated, may hold values from 0.5 to 1.5
- w_qkv: bfloat16 [768, 2304], replicated, may hold values from -0.21875 to 0.21875
- conv_taps: bfloat16 [3, 2304], replicated, may hold values from -3 to 3
- w_out: bfloat16 [768, 768], replicated, may hold values from -1.75 to 1.75
- norm2_gain: bfloat16 [768], replicated, may hold values from 0.5 to 1.5
- w_up: bfloat16 [768, 3072], replicated, may hold values from -0.21875 to 0.21875
- w_down: bfloat16 [3072, 768], replicated, may hold values from -0.109375 to 0.109375
- grad_output: bfloat16 [16, 2048, 768], P('batch', 'seq'), may hold values from -6 to 6
Outputs:
- stream_out: bfloat16 [16, 2048, 768], P('batch', 'seq')
- grad_input: float32 [16, 2048, 768], P('batch', 'seq')
- grad_norm1: float32 [768], P('batch')
- grad_qkv: float32 [768, 2304], P('batch')
- grad_taps: float32 [3, 2304], replicated
- grad_wout: float32 [768, 768], P('batch')
- grad_norm2: float32 [768], P('batch')
- grad_up: float32 [768, 3072], P('batch')
- grad_down: float32 [3072, 768], P('batch')
- block_rms: float32 [3], replicated
Inputs may be any that keep to these rules, and one draw needn't show every extreme that they name: `lengths`: lengths are heavy tailed over 64 to 2048; some sequence has exactly 2048. `token_mask`: 0 or 1; the first position of every sequence is 1.
All inputs are finite; a program needn't handle non-finite values.
Results may differ from a plain program's by a relative error of at most 0.02.
Values may be sent and summed in bfloat16 or wider, within the bound.
A program may use at most 384 MiB of HBM per device.

v0:
```python
import math
import jax
import jax.numpy as jnp
from jax import lax
from jax.sharding import PartitionSpec as P

HEADS = 12
HEAD = 64


def from_behind(value, axis, steps):
    count = lax.axis_size(axis)
    initial, last = (max(0, -steps), min(count, count - steps))
    return lax.ppermute(value, axis, [(source, source + steps) for source in range(initial, last)])


def dense(left_op, right_op):
    return jnp.dot(left_op, right_op, preferred_element_type=jnp.float32)


def norm_forward(values, gain_vec):
    factor = lax.rsqrt(jnp.mean(values * values, axis=-1, keepdims=True) + 1e-06)
    return (values * factor * gain_vec, factor)


def norm_backward(values, factor, gain_vec, upstream):
    weighted = upstream * gain_vec
    inner_mean = jnp.mean(weighted * values, axis=-1, keepdims=True)
    d_values = factor * weighted - values * (factor * factor * factor) * inner_mean
    d_gain = jnp.sum(upstream * values * factor, axis=(0, 1))
    return (d_values, d_gain)


def split_heads(row_block):
    return row_block.reshape(row_block.shape[0], HEADS, HEAD)


def score_block(q_rows, k_rows, q_begin, k_begin, length):
    factor = 1.0 / math.sqrt(HEAD)
    scores = (
        jnp.einsum(
            "qhe,khe->hqk",
            split_heads(q_rows),
            split_heads(k_rows),
            preferred_element_type=jnp.float32,
        )
        * factor
    )
    q_pos = q_begin + jnp.arange(q_rows.shape[0], dtype=jnp.int32)
    k_pos = k_begin + jnp.arange(k_rows.shape[0], dtype=jnp.int32)
    allowed = (k_pos[None, :] <= q_pos[:, None]) & (k_pos[None, :] < length)
    return (scores, allowed[None])


def attend_forward(q_rows, k_rows, v_rows, length, offset):
    scores, allowed = score_block(q_rows, k_rows, offset, 0, length)
    masked = jnp.where(allowed, scores, -1e30)
    row_max = jnp.max(masked, axis=-1, keepdims=True)
    exp_terms = jnp.exp(masked - row_max)
    row_total = jnp.sum(exp_terms, axis=-1, keepdims=True)
    weights = (exp_terms / row_total).astype(jnp.bfloat16)
    attended = jnp.einsum(
        "hqk,khe->qhe", weights, split_heads(v_rows), preferred_element_type=jnp.float32
    )
    return (attended.reshape(q_rows.shape[0], HEADS * HEAD), (row_max + jnp.log(row_total))[..., 0])


def attend_backward(q_rows, k_rows, v_rows, d_rows, log_total, length, offset):
    scores, allowed = score_block(q_rows, k_rows, offset, 0, length)
    prob_rows = jnp.where(allowed, jnp.exp(scores - log_total[..., None]), 0.0)
    d_probs = jnp.einsum(
        "qhe,khe->hqk", split_heads(d_rows), split_heads(v_rows), preferred_element_type=jnp.float32
    )
    delta_rows = jnp.sum(prob_rows * d_probs, axis=-1, keepdims=True)
    d_scores = (prob_rows * (d_probs - delta_rows)).astype(jnp.bfloat16)
    factor = 1.0 / math.sqrt(HEAD)
    d_query = (
        jnp.einsum(
            "hqk,khe->qhe", d_scores, split_heads(k_rows), preferred_element_type=jnp.float32
        ).reshape(q_rows.shape[0], HEADS * HEAD)
        * factor
    )
    return (d_query, d_scores, prob_rows, delta_rows[..., 0])


def shards(
    stream_in,
    lengths,
    token_mask,
    norm1_gain,
    w_qkv,
    conv_taps,
    w_out,
    norm2_gain,
    w_up,
    w_down,
    grad_output,
):
    seq_count, block_len, model_width = stream_in.shape
    offset = lax.axis_index("seq") * block_len
    factor = 1.0 / math.sqrt(HEAD)
    gain_one = norm1_gain.astype(jnp.float32)
    gain_two = norm2_gain.astype(jnp.float32)
    taps = conv_taps.astype(jnp.float32)
    resid = stream_in.astype(jnp.float32)
    positions = offset + jnp.arange(block_len, dtype=jnp.int32)
    stat_weight = token_mask.astype(jnp.float32) * (positions[None, :] < lengths[:, None]).astype(
        jnp.float32
    )
    cotangent = (grad_output.astype(jnp.float32) * stat_weight[..., None]).astype(jnp.bfloat16)
    normed1, factor_one = norm_forward(resid, gain_one)
    normed1_low = normed1.astype(jnp.bfloat16)
    projected = dense(normed1_low, w_qkv)
    rim_rows = from_behind(projected[:, block_len - 2 :], "seq", 1)
    extended = jnp.concatenate([rim_rows, projected], axis=1)
    mixed = (
        taps[0] * extended[:, 2:]
        + taps[1] * extended[:, 1 : block_len + 1]
        + taps[2] * extended[:, :block_len]
    ).astype(jnp.bfloat16)
    query = mixed[..., :model_width]
    keys_own = mixed[..., model_width : 2 * model_width]
    values_own = mixed[..., 2 * model_width :]
    keys_all, values_all = (
        lax.all_gather(keys_own, "seq", axis=1, tiled=True),
        lax.all_gather(values_own, "seq", axis=1, tiled=True),
    )

    def forward_one(item):
        return attend_forward(item[0], item[1], item[2], item[3], offset)

    attended, log_totals = lax.map(forward_one, (query, keys_all, values_all, lengths))
    attended_low = attended.astype(jnp.bfloat16)
    branch_attn = dense(attended_low, w_out)
    hidden1 = resid + branch_attn
    normed2, factor_two = norm_forward(hidden1, gain_two)
    normed2_low = normed2.astype(jnp.bfloat16)
    up_proj = dense(normed2_low, w_up)
    active = jax.nn.relu(up_proj)
    squared = (active * active).astype(jnp.bfloat16)
    branch_ff = dense(squared, w_down)
    stream_full = hidden1 + branch_ff
    stream_out = stream_full.astype(jnp.bfloat16)

    def masked_square(values):
        return jnp.sum(stat_weight * jnp.sum(values * values, axis=-1))

    local_stats = jnp.stack(
        [
            masked_square(stream_full),
            masked_square(branch_attn),
            masked_square(branch_ff),
            jnp.sum(stat_weight),
        ]
    )
    grad_down = jnp.einsum("scf,scd->fd", squared, cotangent, preferred_element_type=jnp.float32)
    d_squared = jnp.einsum("scd,fd->scf", cotangent, w_down, preferred_element_type=jnp.float32)
    d_up = (2.0 * active * d_squared).astype(jnp.bfloat16)
    grad_up = jnp.einsum("scd,scf->df", normed2_low, d_up, preferred_element_type=jnp.float32)
    d_normed2 = jnp.einsum("scf,df->scd", d_up, w_up, preferred_element_type=jnp.float32)
    d_hidden_norm, grad_norm2 = norm_backward(hidden1, factor_two, gain_two, d_normed2)
    d_hidden1 = cotangent.astype(jnp.float32) + d_hidden_norm
    d_attn = d_hidden1.astype(jnp.bfloat16)
    grad_wout = jnp.einsum("scd,sce->de", attended_low, d_attn, preferred_element_type=jnp.float32)
    d_attended = jnp.einsum(
        "sce,de->scd", d_attn, w_out, preferred_element_type=jnp.float32
    ).astype(jnp.bfloat16)

    def backward_local(item):
        d_query, d_scores, prob_rows, delta_rows = attend_backward(
            item[0], item[1], item[2], item[3], item[4], item[5], offset
        )
        return (d_query, delta_rows)

    d_query_all, delta_all = lax.map(
        backward_local, (query, keys_all, values_all, d_attended, log_totals, lengths)
    )
    lse_rows, delta_rows_all = (
        lax.all_gather(log_totals, "seq", axis=2, tiled=True),
        lax.all_gather(delta_all, "seq", axis=2, tiled=True),
    )
    begin_row = jnp.int32(0)
    q_piece = lax.all_gather(query, "seq", axis=1, tiled=True)
    d_piece = lax.all_gather(d_attended, "seq", axis=1, tiled=True)

    def per_sequence(q_rows, d_rows, k_rows, v_rows, lse_seq, delta_seq, length):
        scores, allowed = score_block(q_rows, k_rows, begin_row, offset, length)
        prob_rows = jnp.where(allowed, jnp.exp(scores - lse_seq[..., None]), 0.0)
        d_probs = jnp.einsum(
            "qhe,khe->hqk",
            split_heads(d_rows),
            split_heads(v_rows),
            preferred_element_type=jnp.float32,
        )
        d_scores = (prob_rows * (d_probs - delta_seq[..., None])).astype(jnp.bfloat16)
        d_keys_part = (
            jnp.einsum(
                "hqk,qhe->khe", d_scores, split_heads(q_rows), preferred_element_type=jnp.float32
            ).reshape(k_rows.shape[0], model_width)
            * factor
        )
        d_values_part = jnp.einsum(
            "hqk,qhe->khe",
            prob_rows.astype(jnp.bfloat16),
            split_heads(d_rows),
            preferred_element_type=jnp.float32,
        ).reshape(k_rows.shape[0], model_width)
        return (d_keys_part, d_values_part)

    d_keys_part, d_values_part = jax.vmap(per_sequence)(
        q_piece, d_piece, keys_own, values_own, lse_rows, delta_rows_all, lengths
    )
    d_mixed = jnp.concatenate([d_query_all, d_keys_part, d_values_part], axis=-1)
    rim_terms = jnp.stack(
        [taps[2] * d_mixed[:, 0], taps[1] * d_mixed[:, 0] + taps[2] * d_mixed[:, 1]], axis=1
    )
    back_rows = from_behind(rim_terms.astype(jnp.bfloat16), "seq", -1).astype(rim_terms.dtype)
    padded = jnp.concatenate(
        [d_mixed, jnp.zeros((seq_count, 2, 3 * model_width), jnp.float32)], axis=1
    )
    d_proj = (
        taps[0] * padded[:, :block_len]
        + taps[1] * padded[:, 1 : block_len + 1]
        + taps[2] * padded[:, 2:]
    )
    d_proj = d_proj + jnp.pad(back_rows, ((0, 0), (block_len - 2, 0), (0, 0)))
    d_proj_low = d_proj.astype(jnp.bfloat16)
    grad_taps = jnp.stack(
        [
            jnp.sum(d_mixed * extended[:, 2:], axis=(0, 1)),
            jnp.sum(d_mixed * extended[:, 1 : block_len + 1], axis=(0, 1)),
            jnp.sum(d_mixed * extended[:, :block_len], axis=(0, 1)),
        ]
    )
    grad_qkv = jnp.einsum(
        "scd,scn->dn", normed1_low, d_proj_low, preferred_element_type=jnp.float32
    )
    d_normed1 = jnp.einsum("scn,dn->scd", d_proj_low, w_qkv, preferred_element_type=jnp.float32)
    d_input_norm, grad_norm1 = norm_backward(resid, factor_one, gain_one, d_normed1)
    grad_input = d_hidden1 + d_input_norm
    shares = (
        lax.psum_scatter(
            grad_norm1.astype(jnp.bfloat16), "batch", scatter_dimension=0, tiled=True
        ).astype(jnp.float32),
        lax.psum_scatter(
            grad_qkv.astype(jnp.bfloat16), "batch", scatter_dimension=0, tiled=True
        ).astype(jnp.float32),
        lax.psum_scatter(
            grad_wout.astype(jnp.bfloat16), "batch", scatter_dimension=0, tiled=True
        ).astype(jnp.float32),
        lax.psum_scatter(
            grad_norm2.astype(jnp.bfloat16), "batch", scatter_dimension=0, tiled=True
        ).astype(jnp.float32),
        lax.psum_scatter(
            grad_up.astype(jnp.bfloat16), "batch", scatter_dimension=0, tiled=True
        ).astype(jnp.float32),
        lax.psum_scatter(
            grad_down.astype(jnp.bfloat16), "batch", scatter_dimension=0, tiled=True
        ).astype(jnp.float32),
    )
    totals = (
        lax.psum(shares[0].astype(jnp.bfloat16), "seq").astype(jnp.float32),
        lax.psum(shares[1].astype(jnp.bfloat16), "seq").astype(jnp.float32),
        lax.psum(shares[2].astype(jnp.bfloat16), "seq").astype(jnp.float32),
        lax.psum(shares[3].astype(jnp.bfloat16), "seq").astype(jnp.float32),
        lax.psum(shares[4].astype(jnp.bfloat16), "seq").astype(jnp.float32),
        lax.psum(shares[5].astype(jnp.bfloat16), "seq").astype(jnp.float32),
    )
    small = lax.psum((grad_taps, local_stats), ("seq", "batch"))
    block_rms = jnp.sqrt(small[1][:3] / (model_width * small[1][3]))
    return (
        stream_out,
        grad_input,
        totals[0],
        totals[1],
        small[0],
        totals[2],
        totals[3],
        totals[4],
        totals[5],
        block_rms,
    )


def solution(mesh):
    return jax.shard_map(
        shards,
        mesh=mesh,
        in_specs=(
            P("batch", "seq", None),
            P("batch"),
            P("batch", "seq"),
            P(),
            P(),
            P(),
            P(),
            P(),
            P(),
            P(),
            P("batch", "seq", None),
        ),
        out_specs=(
            P("batch", "seq", None),
            P("batch", "seq", None),
            P("batch"),
            P("batch", None),
            P(),
            P("batch", None),
            P("batch"),
            P("batch", None),
            P("batch", None),
            P(),
        ),
        check_vma=False,
    )
```

profile of v0, /device:TPU:0, one launch (start us, length us, event | category | flops | bytes accessed | tf_op | source)
XLA Modules:
  0.0 1237.5 jit_solution(3690341579583954142)
XLA Ops:
  23.6 13.4 %constant_dynamic-update-slice_fusion.1 = f32[4,258,2304]{2,0,1:T(4,128)} fusion(f32[4,258,2304]{2,0,1:T(4,128)} %constant_dynamic-update-slice_fusion.2, f32[4,256,2304]{2,1,0:T(8,128)} %copy-done.2), kind=kLoop, calls=%fused_computation.113 | loop fusion | bytes 18874368 | tf_op jit(solution)/shard_map/concatenate | solution.py:115
  37.0 17.5 %add_convert_fusion.1 = bf16[4,256,2304]{2,0,1:T(4,128)(2,1)S(1)} fusion(f32[4,258,2304]{2,0,1:T(4,128)} %constant_dynamic-update-slice_fusion.1, f32[2304]{0:T(1024)S(1)} %get-tuple-element.212, f32[2304]{0:T(1024)} %get-tuple-element.213, f32[2304]{0:T(1024)} %get-tuple-element.211, f32[4,256,2304]{2,1,0:T(8,128)} %copy-done.2), kind=kLoop, calls=%fused_computation.52 | loop fusion | flops 14155776 | bytes 33057792 | tf_op jit(solution)/shard_map/convert_element_type | solution.py:120
  64.8 70.0 %all-gather.7.cloned.1.call-done = bf16[4,2048,768]{2,0,1:T(4,128)(2,1)} async-done(((bf16[4,256,768]{2,0,1:T(4,128)(2,1)}), bf16[4,2048,768]{2,0,1:T(4,128)(2,1)}) %all-gather.7.cloned.1.call-update) | async-done | bytes 12582928 | tf_op jit(solution)/shard_map/all_gather | solution.py:125
  134.8 20.3 %copy.104 = bf16[4,2048,768]{1,2,0:T(8,128)(2,1)} copy(bf16[4,2048,768]{2,0,1:T(4,128)(2,1)} %all-gather.7.cloned.1.call-done) | data formatting | bytes 25165824 | tf_op jit(solution)/shard_map/while | solution.py:132
  155.1 53.8 %all-gather.5.cloned.1.call-done = bf16[4,2048,768]{2,0,1:T(4,128)(2,1)} async-done(((bf16[4,256,768]{2,0,1:T(4,128)(2,1)}), bf16[4,2048,768]{2,0,1:T(4,128)(2,1)}) %all-gather.5.cloned.1.call-update) | async-done | bytes 12582928 | tf_op jit(solution)/shard_map/all_gather | solution.py:126
  208.9 20.3 %copy.102 = bf16[4,2048,768]{1,2,0:T(8,128)(2,1)} copy(bf16[4,2048,768]{2,0,1:T(4,128)(2,1)} %all-gather.5.cloned.1.call-done) | data formatting | bytes 25165824 | tf_op jit(solution)/shard_map/while | solution.py:132
  229.8 170.0 %while.24 = (s32[]{:T(128)}, bf16[4,256,768]{1,2,0:T(8,128)(2,1)}, f32[4,12,256]{2,1,0:T(8,128)}, bf16[4,2048,768]{1,2,0:T(8,128)(2,1)}, s32[]{:T(128)}, /*index...) while((s32[]{:T(128)}, bf16[4,256,768]{1,2,0:T(8,128)(2,1)}, ...), condition=%wide.region_4.5_spmd, body=%wide.region_1.4_spmd.sunk | while | flops 1687158016 | bytes 98936960 | solution.py:132
  236.5 12.3 fusion.108
  248.9 11.6 fusion.109
  260.5 12.0 fusion.110
  280.6 10.5 fusion.108
  291.1 11.5 fusion.109
  302.7 11.8 fusion.110
  322.6 10.5 fusion.108
  333.1 11.5 fusion.109
  344.7 11.8 fusion.110
  364.6 10.5 fusion.108
  375.1 11.5 fusion.109
  386.7 11.8 fusion.110
  430.5 10.5 multiply_reduce_fusion.6
  463.7 10.4 bitcast_convert_fusion
  474.8 350.4 %while.25 = (s32[]{:T(128)}, f32[4,256,768]{2,0,1:T(4,128)}, f32[4,12,256]{2,1,0:T(8,128)}, bf16[4,2048,768]{1,2,0:T(8,128)(2,1)}, s32[]{:T(128)}, /*index=5*/s3...) while((s32[]{:T(128)}, f32[4,256,768]{2,0,1:T(4,128)}, ...), condition=%wide.region_9.10_spmd, body=%wide.region_7.9_spmd.sunk | while | flops 2486369536 | bytes 169195712 | solution.py:175
  492.4 10.3 fusion.116
  502.7 19.8 %multiply_reduce_fusion.14 = (f32[12,256]{1,0:T(8,128)}, f32[12,256,2048]{2,1,0:T(8,128)}) fusion(f32[12,256,2048]{2,1,0:T(8,128)} %fusion.116, f32[12,256]{1,0:T(8,128)S(1)} %dynamic-slice_bitcast_fusion.2, pred[256,2048]{1,0:T(8,128)(4,1)} %fusion.117, bf16[256,12,64]{0,2,1:T(8,128)(2,1)} %bitcast.149, bf16[2048,12,64]{0,2,1:T(8,128)(2,1)} %bitcast.142), kind=kOutput, calls=%fused_computation.18.clone.1 | convolution fusion | flops 836760576 | bytes 54419456 | tf_op jit(solution)/shard_map/while/body/eval_jaxpr/qhe,khe->hqk/dot_general | solution.py:71
  522.5 20.4 %fusion.118 = f32[12,64,256]{2,1,0:T(8,128)} fusion(bf16[2048,12,64]{0,2,1:T(8,128)(2,1)} %bitcast.140, f32[12,256,2048]{2,1,0:T(8,128)} %get-tuple-element.413, f32[12,256,2048]{2,1,0:T(8,128)} %fusion.116, f32[12,256]{1,0:T(8,128)} %get-tuple-element.414, f32[12,256]{1,0:T(8,128)S(1)} %dynamic-slice_bitcast_fusion.2, pred[256,2048]{1,0:T(8,128)(4,1)} %fusion.117), kind=kOutput, calls=%fused_computation.24.clone.1 | convolution fusion | flops 843251712 | bytes 54812672 | tf_op jit(solution)/shard_map/while/body/eval_jaxpr/hqk,khe->qhe/dot_general | solution.py:78
  547.3 15.6 %dynamic_update_slice.24 = f32[4,256,768]{2,0,1:T(4,128)} dynamic-update-slice(f32[4,256,768]{2,0,1:T(4,128)} %get-tuple-element.455, f32[1,256,768]{2,0,1:T(1,128)} %copy.160, s32[]{:T(128)S(6)} %copy.178, s32[]{:T(128)} %constant.66.clone.1..sunk, s32[]{:T(128)} %constant.66.clone.1..sunk) | dynamic-update-slice | bytes 1572868 | tf_op jit(solution)/shard_map/while/body/jit(dynamic_update_index_in_dim)/dynamic_update_slice | solution.py:132
  590.6 19.8 %multiply_reduce_fusion.14 = (f32[12,256]{1,0:T(8,128)}, f32[12,256,2048]{2,1,0:T(8,128)}) fusion(f32[12,256,2048]{2,1,0:T(8,128)} %fusion.116, f32[12,256]{1,0:T(8,128)S(1)} %dynamic-slice_bitcast_fusion.2, pred[256,2048]{1,0:T(8,128)(4,1)} %fusion.117, bf16[256,12,64]{0,2,1:T(8,128)(2,1)} %bitcast.149, bf16[2048,12,64]{0,2,1:T(8,128)(2,1)} %bitcast.142), kind=kOutput, calls=%fused_computation.18.clone.1 | convolution fusion | flops 836760576 | bytes 54419456 | tf_op jit(solution)/shard_map/while/body/eval_jaxpr/qhe,khe->hqk/dot_general | solution.py:71
  610.4 20.3 %fusion.118 = f32[12,64,256]{2,1,0:T(8,128)} fusion(bf16[2048,12,64]{0,2,1:T(8,128)(2,1)} %bitcast.140, f32[12,256,2048]{2,1,0:T(8,128)} %get-tuple-element.413, f32[12,256,2048]{2,1,0:T(8,128)} %fusion.116, f32[12,256]{1,0:T(8,128)} %get-tuple-element.414, f32[12,256]{1,0:T(8,128)S(1)} %dynamic-slice_bitcast_fusion.2, pred[256,2048]{1,0:T(8,128)(4,1)} %fusion.117), kind=kOutput, calls=%fused_computation.24.clone.1 | convolution fusion | flops 843251712 | bytes 54812672 | tf_op jit(solution)/shard_map/while/body/eval_jaxpr/hqk,khe->qhe/dot_general | solution.py:78
  635.1 15.5 %dynamic_update_slice.24 = f32[4,256,768]{2,0,1:T(4,128)} dynamic-update-slice(f32[4,256,768]{2,0,1:T(4,128)} %get-tuple-element.455, f32[1,256,768]{2,0,1:T(1,128)} %copy.160, s32[]{:T(128)S(6)} %copy.178, s32[]{:T(128)} %constant.66.clone.1..sunk, s32[]{:T(128)} %constant.66.clone.1..sunk) | dynamic-update-slice | bytes 1572868 | tf_op jit(solution)/shard_map/while/body/jit(dynamic_update_index_in_dim)/dynamic_update_slice | solution.py:132
  678.2 19.8 %multiply_reduce_fusion.14 = (f32[12,256]{1,0:T(8,128)}, f32[12,256,2048]{2,1,0:T(8,128)}) fusion(f32[12,256,2048]{2,1,0:T(8,128)} %fusion.116, f32[12,256]{1,0:T(8,128)S(1)} %dynamic-slice_bitcast_fusion.2, pred[256,2048]{1,0:T(8,128)(4,1)} %fusion.117, bf16[256,12,64]{0,2,1:T(8,128)(2,1)} %bitcast.149, bf16[2048,12,64]{0,2,1:T(8,128)(2,1)} %bitcast.142), kind=kOutput, calls=%fused_computation.18.clone.1 | convolution fusion | flops 836760576 | bytes 54419456 | tf_op jit(solution)/shard_map/while/body/eval_jaxpr/qhe,khe->hqk/dot_general | solution.py:71
  697.9 20.1 %fusion.118 = f32[12,64,256]{2,1,0:T(8,128)} fusion(bf16[2048,12,64]{0,2,1:T(8,128)(2,1)} %bitcast.140, f32[12,256,2048]{2,1,0:T(8,128)} %get-tuple-element.413, f32[12,256,2048]{2,1,0:T(8,128)} %fusion.116, f32[12,256]{1,0:T(8,128)} %get-tuple-element.414, f32[12,256]{1,0:T(8,128)S(1)} %dynamic-slice_bitcast_fusion.2, pred[256,2048]{1,0:T(8,128)(4,1)} %fusion.117), kind=kOutput, calls=%fused_computation.24.clone.1 | convolution fusion | flops 843251712 | bytes 54812672 | tf_op jit(solution)/shard_map/while/body/eval_jaxpr/hqk,khe->qhe/dot_general | solution.py:78
  722.4 15.5 %dynamic_update_slice.24 = f32[4,256,768]{2,0,1:T(4,128)} dynamic-update-slice(f32[4,256,768]{2,0,1:T(4,128)} %get-tuple-element.455, f32[1,256,768]{2,0,1:T(1,128)} %copy.160, s32[]{:T(128)S(6)} %copy.178, s32[]{:T(128)} %constant.66.clone.1..sunk, s32[]{:T(128)} %constant.66.clone.1..sunk) | dynamic-update-slice | bytes 1572868 | tf_op jit(solution)/shard_map/while/body/jit(dynamic_update_index_in_dim)/dynamic_update_slice | solution.py:132
  765.5 19.8 %multiply_reduce_fusion.14 = (f32[12,256]{1,0:T(8,128)}, f32[12,256,2048]{2,1,0:T(8,128)}) fusion(f32[12,256,2048]{2,1,0:T(8,128)} %fusion.116, f32[12,256]{1,0:T(8,128)S(1)} %dynamic-slice_bitcast_fusion.2, pred[256,2048]{1,0:T(8,128)(4,1)} %fusion.117, bf16[256,12,64]{0,2,1:T(8,128)(2,1)} %bitcast.149, bf16[2048,12,64]{0,2,1:T(8,128)(2,1)} %bitcast.142), kind=kOutput, calls=%fused_computation.18.clone.1 | convolution fusion | flops 836760576 | bytes 54419456 | tf_op jit(solution)/shard_map/while/body/eval_jaxpr/qhe,khe->hqk/dot_general | solution.py:71
  785.2 20.1 %fusion.118 = f32[12,64,256]{2,1,0:T(8,128)} fusion(bf16[2048,12,64]{0,2,1:T(8,128)(2,1)} %bitcast.140, f32[12,256,2048]{2,1,0:T(8,128)} %get-tuple-element.413, f32[12,256,2048]{2,1,0:T(8,128)} %fusion.116, f32[12,256]{1,0:T(8,128)} %get-tuple-element.414, f32[12,256]{1,0:T(8,128)S(1)} %dynamic-slice_bitcast_fusion.2, pred[256,2048]{1,0:T(8,128)(4,1)} %fusion.117), kind=kOutput, calls=%fused_computation.24.clone.1 | convolution fusion | flops 843251712 | bytes 54812672 | tf_op jit(solution)/shard_map/while/body/eval_jaxpr/hqk,khe->qhe/dot_general | solution.py:78
  809.7 15.5 %dynamic_update_slice.24 = f32[4,256,768]{2,0,1:T(4,128)} dynamic-update-slice(f32[4,256,768]{2,0,1:T(4,128)} %get-tuple-element.455, f32[1,256,768]{2,0,1:T(1,128)} %copy.160, s32[]{:T(128)S(6)} %copy.178, s32[]{:T(128)} %constant.66.clone.1..sunk, s32[]{:T(128)} %constant.66.clone.1..sunk) | dynamic-update-slice | bytes 1572868 | tf_op jit(solution)/shard_map/while/body/jit(dynamic_update_index_in_dim)/dynamic_update_slice | solution.py:132
  825.2 10.9 all_gather.21
  836.1 11.3 all_gather.23
  857.3 20.1 %copy.110 = bf16[4,2048,768]{1,2,0:T(8,128)(2,1)} copy(bf16[4,2048,768]{2,0,1:T(4,128)(2,1)} %all-gather.9.cloned.1.call-done) | data formatting | bytes 25165824 | tf_op jit(solution)/shard_map/all_gather | solution.py:183
  877.5 39.7 %fusion.62 = f32[4,12,2048,256]{3,2,1,0:T(8,128)} fusion(bf16[4,2048,12,64]{1,3,2,0:T(8,128)(2,1)} %bitcast.147, bf16[4,256,12,64]{1,3,2,0:T(8,128)(2,1)} %bitcast.153), kind=kOutput, calls=%fused_computation.137 | convolution fusion | flops 3221225472 | bytes 114819072 | tf_op jit(solution)/shard_map/vmap(qhe,khe->hqk)/dot_general | solution.py:41
  917.2 16.0 %copy.112 = bf16[4,2048,768]{1,2,0:T(8,128)(2,1)} copy(bf16[4,2048,768]{2,1,0:T(8,128)(2,1)} %all-gather.11.cloned.1.call-done) | data formatting | bytes 25165824 | tf_op jit(solution)/shard_map/all_gather | solution.py:184
  933.2 38.9 %fusion.13 = f32[4,12,64,256]{3,2,1,0:T(8,128)} fusion(bf16[4,2048,12,64]{1,3,2,0:T(8,128)(2,1)} %bitcast.150, f32[4,12,2048,256]{3,2,1,0:T(8,128)} %fusion.62, f32[4,12,2048]{2,1,0:T(8,128)} %all_gather.21, pred[4,2048,256]{2,1,0:T(8,128)(4,1)} %broadcast_and_fusion), kind=kOutput, calls=%fused_computation.38 | convolution fusion | flops 3321888768 | bytes 118882304 | tf_op jit(solution)/shard_map/vmap(hqk,qhe->khe)/dot_general | solution.py:202
  977.1 51.0 %fusion.42 = f32[4,12,64,256]{3,2,1,0:T(8,128)} fusion(bf16[4,2048,12,64]{1,3,2,0:T(8,128)(2,1)} %bitcast.148, f32[4,12,2048,256]{3,2,1,0:T(8,128)} %fusion.62, f32[4,12,2048]{2,1,0:T(8,128)} %all_gather.23, f32[4,12,2048]{2,1,0:T(8,128)} %all_gather.21, pred[4,2048,256]{2,1,0:T(8,128)(4,1)} %broadcast_and_fusion, bf16[4,2048,12,64]{1,3,2,0:T(8,128)(2,1)} %bitcast.151, ...), kind=kOutput, calls=%fused_computation.94 | convolution fusion | flops 6594232320 | bytes 133431296 | tf_op jit(solution)/shard_map/vmap(hqk,qhe->khe)/dot_general | solution.py:197
  1033.0 20.5 %multiply_reduce_fusion.2 = (f32[2304]{0:T(1024)}, f32[2304]{0:T(1024)}, f32[2304]{0:T(1024)S(1)}, f32[4,256,2304]{2,0,1:T(4,128)S(1)}) fusion(f32[4,258,2304]{2,0,1:T(4,128)} %constant_dynamic-update-slice_fusion.1, f32[4,256,768]{2,0,1:T(4,128)} %copy.116, f32[4,256,768]{2,0,1:T(4,128)} %copy.115, f32[4,256,768]{2,0,1:T(4,128)} %get-tuple-element.108, ...), kind=kLoop, calls=%fused_computation.49 | loop fusion | flops 18867456 | bytes 47213568 | tf_op jit(solution)/shard_map/reduce_sum | solution.py:231
  1082.8 47.2 %all-reduce.4 = (f32[3,2304]{1,0:T(4,128)}, f32[4]{0:T(128)S(1)}) all-reduce(f32[3,2304]{1,0:T(4,128)} %pad_maximum_fusion.2, f32[4]{0:T(128)} %pad_maximum_fusion.3), channel_id=1, replica_groups=mesh['seq'=8,'batch'=4] {'seq','batch'}, use_global_device_ids=true, to_apply=%region_19.20 | all-reduce | flops 6916 | bytes 55328 | tf_op jit(solution)/shard_map/psum | solution.py:269
  1131.3 13.2 %reduce-scatter.5.cloned.1.call-done = bf16[192,2304]{1,0:T(8,128)(2,1)} async-done(((bf16[768,2304]{1,0:T(8,128)(2,1)}), bf16[192,2304]{1,0:T(8,128)(2,1)}) %reduce-scatter.5.cloned.1.call-update) | async-done | bytes 884752 | tf_op jit(solution)/shard_map/reduce_scatter | solution.py:245
  1154.2 11.5 all-reduce.7
  1167.7 12.5 %all-reduce.5 = (bf16[192]{0:T(256)(128)(2,1)}, bf16[192]{0:T(256)(128)(2,1)}) all-reduce(bf16[192]{0:T(256)(128)(2,1)S(1)} %dynamic-slice.1, bf16[192]{0:T(256)(128)(2,1)} %dynamic-slice.3), channel_id=1, replica_groups=mesh['seq'=8,'batch'=4] {'seq'}, use_global_device_ids=true, to_apply=%region_13.14 | all-reduce | flops 384 | bytes 1536 | tf_op jit(solution)/shard_map/psum | solution.py:262
  1188.3 34.7 %all-reduce.10.cloned.1.call-done = (bf16[192,2304]{1,0:T(8,128)(2,1)}, bf16[192,768]{1,0:T(8,128)(2,1)}, bf16[192,3072]{1,0:T(8,128)(2,1)}, bf16[768,768]{1,0:T(8,128)(2,1)}) async-done(((bf16[192,2304]{1,0:T(8,128)(2,1)}, bf16[192,768]{1,0:T(8,128)(2,1)}, bf16[192,3072]{1,0:T(8,128)(2,1)}, bf16[768,768]{1,0:T(8,128)(2,1)}), (bf16[192,2304]{1,0:T(8,128)(2,1)}, bf16[192,768]{1,0:T(8,128)(2,1)}, ...) | async-done | bytes 3538960 | tf_op jit(solution)/shard_map/psum | solution.py:263
  (243 shorter events, 308.0 us)
Async XLA Ops:
  7.2 3.5 copy-start
  7.2 127.6 %all-gather.7.cloned.1.call-start = ((), (), s32[]{:S(2)}) async-start(), calls=%async_computation.5 | async-start | bytes 14155776 | tf_op jit(solution)/shard_map/all_gather | solution.py:125
  8.1 8.0 copy-start.23
  10.7 5.4 copy-start.20
  10.7 11.6 copy-start.16
  16.1 3.6 copy-start.2
  19.7 3.3 collective-permute-start
  22.9 14.0 %copy-start.10 = (f32[2304]{0:T(1024)}, f32[2304]{0:T(1024)S(1)}, u32[]{:S(2)}) copy-start(f32[2304]{0:T(1024)S(1)} %get-tuple-element.212) | copy-start | bytes 27652
  54.5 3.7 copy-start.30
  54.5 4.9 copy-start.29
  57.4 151.4 %all-gather.5.cloned.1.call-start = ((), (), s32[]{:S(2)}) async-start(), calls=%async_computation.4 | async-start | bytes 14155776 | tf_op jit(solution)/shard_map/all_gather | solution.py:126
  58.2 799.2 %all-gather.9.cloned.1.call-start = ((), (), s32[]{:S(2)}) async-start(), calls=%async_computation.6 | async-start | bytes 14155776 | tf_op jit(solution)/shard_map/all_gather | solution.py:183
  64.5 852.7 %all-gather.11.cloned.1.call-start = ((), (), s32[]{:S(2)}) async-start(), calls=%async_computation.7 | async-start | bytes 14155776 | tf_op jit(solution)/shard_map/all_gather | solution.py:184
  399.8 5.1 copy-start.18
  399.8 5.1 copy-start.32
  399.8 13.6 %slice-start = ((s8[4718592]{0:T(1024)(128)(4,1)}), s8[4194304]{0:T(1024)(128)(4,1)S(1)}, s32[]{:S(2)}) async-start(s8[4718592]{0:T(1024)(128)(4,1)} %bitcast.157), calls=%async_computation.13 | async-start | bytes 8388608
  404.9 36.1 %copy-start.6 = (f32[4,256,768]{2,1,0:T(8,128)}, f32[4,256,768]{2,1,0:T(8,128)S(1)}, u32[]{:S(2)}) copy-start(f32[4,256,768]{2,1,0:T(8,128)S(1)} %get-tuple-element.267) | copy-start | bytes 9437188
  404.9 36.1 %copy-start.17 = (f32[4,256]{1,0:T(4,128)}, f32[4,256]{1,0:T(4,128)S(1)}, u32[]{:S(2)}) copy-start(f32[4,256]{1,0:T(4,128)S(1)} %get-tuple-element.287) | copy-start | bytes 12292
  404.9 8.5 copy-start.7
  404.9 8.5 copy-start.14
  404.9 8.5 slice-start.1
  441.0 2.8 copy-start.33
  443.7 2.7 copy-start.28
  446.4 684.8 %reduce-scatter.7.cloned.1.call-start = ((), (), s32[]{:S(2)}) async-start(), calls=%async_computation.9 | async-start | bytes 1474560 | tf_op jit(solution)/shard_map/reduce_scatter | solution.py:248
  447.6 5.1 copy-start.26
  452.5 678.8 %reduce-scatter.11.cloned.1.call-start = ((), (), s32[]{:S(2)}) async-start(), calls=%async_computation.11 | async-start | bytes 5898240 | tf_op jit(solution)/shard_map/reduce_scatter | solution.py:257
  474.1 657.1 %reduce-scatter.9.cloned.1.call-start = ((), (), s32[]{:S(2)}) async-start(), calls=%async_computation.10 | async-start | bytes 5898240 | tf_op jit(solution)/shard_map/reduce_scatter | solution.py:254
  490.6 1.8 copy-start.1
  578.7 1.8 copy-start.1
  666.3 1.8 copy-start.1
  753.7 1.8 copy-start.1
  857.3 287.2 %reduce-scatter.5.cloned.1.call-start = ((), (), s32[]{:S(2)}) async-start(), calls=%async_computation.8 | async-start | bytes 4423680 | tf_op jit(solution)/shard_map/reduce_scatter | solution.py:245
  1033.0 20.5 %copy-start.11 = (f32[2304]{0:T(1024)S(1)}, f32[2304]{0:T(1024)}, u32[]{:S(2)}) copy-start(f32[2304]{0:T(1024)} %copy-done.10) | copy-start | bytes 27652
  1033.0 20.5 %copy-start.12 = (f32[2304]{0:T(1024)S(1)}, f32[2304]{0:T(1024)}, u32[]{:S(2)}) copy-start(f32[2304]{0:T(1024)} %get-tuple-element.213) | copy-start | bytes 27652
  1033.0 24.4 %copy-start.13 = (f32[2304]{0:T(1024)S(1)}, f32[2304]{0:T(1024)}, u32[]{:S(2)}) copy-start(f32[2304]{0:T(1024)} %get-tuple-element.211) | copy-start | bytes 27652
  1053.6 15.0 %copy-start.4 = (bf16[4,256,768]{2,1,0:T(8,128)(2,1)S(1)}, bf16[4,256,768]{2,1,0:T(8,128)(2,1)}, u32[]{:S(2)}) copy-start(bf16[4,256,768]{2,1,0:T(8,128)(2,1)} %param.15) | copy-start | bytes 4718596
  1053.6 15.0 %copy-start.21 = (f32[4,256]{1,0:T(4,128)S(1)}, f32[4,256]{1,0:T(4,128)}, u32[]{:S(2)}) copy-start(f32[4,256]{1,0:T(4,128)} %copy-done.20) | copy-start | bytes 12292
  1053.6 15.0 %copy-start.24 = (f32[768]{0:T(1024)S(1)}, f32[768]{0:T(1024)}, u32[]{:S(2)}) copy-start(f32[768]{0:T(1024)} %copy-done.23) | copy-start | bytes 9220
  1053.7 3.8 collective-permute-start.1
  1066.5 2.1 copy-start.5
  1074.2 2.0 copy-start.15
  1074.2 148.8 %all-reduce.10.cloned.1.call-start = ((), (), s32[]{:S(2)}) async-start(), calls=%async_computation.12 | async-start | bytes 7077888 | tf_op jit(solution)/shard_map/psum | solution.py:263
  1077.5 67.5 %copy-start.22 = (f32[4,256]{1,0:T(4,128)S(1)}, f32[4,256]{1,0:T(4,128)}, u32[]{:S(2)}) copy-start(f32[4,256]{1,0:T(4,128)} %copy-done.20) | copy-start | bytes 12292
  1082.1 62.9 %copy-start.25 = (f32[768]{0:T(1024)S(1)}, f32[768]{0:T(1024)}, u32[]{:S(2)}) copy-start(f32[768]{0:T(1024)} %copy-done.23) | copy-start | bytes 9220
  1145.0 9.2 copy-start.31
  1145.0 38.4 %copy-start.19 = (f32[4,256]{1,0:T(4,128)S(1)}, f32[4,256]{1,0:T(4,128)}, u32[]{:S(2)}) copy-start(f32[4,256]{1,0:T(4,128)} %get-tuple-element.284) | copy-start | bytes 12292
  1223.0 4.5 copy-start.9
  1223.0 6.1 copy-start.8
  (2 other events, 2.2 us)
Sparse Core Ops, SparseCore 0:
  57.5 77.2 all-gather.6
  136.7 72.1 all-gather.4
  210.8 72.1 all-gather.8
  446.5 72.1 all-gather.10
  520.9 29.1 reduce-scatter.6
  552.3 83.9 reduce-scatter.10
  857.4 85.4 reduce-scatter.8
  1074.3 70.0 reduce-scatter.4
  1148.1 74.8 all-reduce.9
where the time goes:
time: 1250 us; the launch traced here: 1240 us
  matrix products  510 us (41%)
  local copies, waits for them, and re-layouts  291 us (23%)
  waiting for transfers between devices  175 us (14%)
  other arithmetic  147 us (12%)
  blocking collectives  93.4 us (7%)
  between operations  15.8 us (1%)
    dot_general x9, matrix products, score_block(): jnp.einsum('qhe,khe->hqk', split_heads(q_rows), split_heads(k_rows), pref...  124 us
    dynamic_update_slice x16, local copies, waits for them, and re-layouts, shards(): lax.map(forward_one, (query, keys_all, values_all, lengths))  82.7 us
    dot_general x4, matrix products, attend_backward(): jnp.einsum('hqk,khe->qhe', d_scores, split_heads(k_rows), preferred_eleme...  81 us
    dot_general x4, matrix products, attend_backward(): jnp.einsum('qhe,khe->hqk', split_heads(d_rows), split_heads(v_rows), pref...  79.1 us
    all_gather x1, waiting for transfers between devices, shards(): lax.all_gather(keys_own, 'seq', axis=1, tiled=True)  70 us
    dynamic_slice x32, local copies, waits for them, and re-layouts, shards(): lax.map(forward_one, (query, keys_all, values_all, lengths))  68.3 us
    all_gather x1, waiting for transfers between devices, shards(): lax.all_gather(values_own, 'seq', axis=1, tiled=True)  53.8 us
    dot_general x1, matrix products, per_sequence(): jnp.einsum('hqk,qhe->khe', d_scores, split_heads(q_rows), preferred_eleme...  51 us
  transfers between devices with their start and end apart: 11, of which 5 were waited for; matrix products, arithmetic and copies ran while one was open for 71% of the time, Pallas kernels for 0%

commit v1 on v0

--- a/solution.py
+++ b/solution.py
@@ -6,6 +6,11 @@
 
 HEADS = 12
 HEAD = 64
+
+
+def gather_and_add(x, mesh_axis):
+    parts = lax.all_gather(x, mesh_axis)
+    return jnp.sum(parts, axis=0)
 
 
 def from_behind(value, axis, steps):
@@ -260,7 +265,7 @@
     )
     totals = (
         lax.psum(shares[0].astype(jnp.bfloat16), "seq").astype(jnp.float32),
-        lax.psum(shares[1].astype(jnp.bfloat16), "seq").astype(jnp.float32),
+        gather_and_add(shares[1].astype(jnp.bfloat16), "seq").astype(jnp.float32),
         lax.psum(shares[2].astype(jnp.bfloat16), "seq").astype(jnp.float32),
         lax.psum(shares[3].astype(jnp.bfloat16), "seq").astype(jnp.float32),
         lax.psum(shares[4].astype(jnp.bfloat16), "seq").astype(jnp.float32),

time: 1250 us -> 1330 us (1.064)
  waiting for transfers between devices: 175 us -> 259 us
    reduce_scatter x1, waiting for transfers between devices: 13.2 us -> 68.8 us  [shards(): lax.psum_scatter(grad_qkv.astype(jnp.bfloat16), 'batch', scatter_dimensio...]
    psum x1, waiting for transfers between devices: 34.7 us -> 63.3 us  [shards(): lax.psum(shares[2].astype(jnp.bfloat16), 'seq').astype(jnp.float32)]
  transfers between devices with their start and end apart: 11 -> 12, of which waited for: 5 -> 5; matrix products, arithmetic and copies ran while one was open for 71% -> 67% of each run, Pallas kernels for 0% -> 0%
where the time goes in v1:
time: 1330 us; the launch traced here: 1320 us
  matrix products  511 us (38%)
  local copies, waits for them, and re-layouts  290 us (22%)
  waiting for transfers between devices  259 us (19%)
  other arithmetic  153 us (12%)
  blocking collectives  86.6 us (7%)
  between operations  16.1 us (1%)
    dot_general x9, matrix products, score_block(): jnp.einsum('qhe,khe->hqk', split_heads(q_rows), split_heads(k_rows), pref...  124 us
    dynamic_update_slice x16, local copies, waits for them, and re-layouts, shards(): lax.map(forward_one, (query, keys_all, values_all, lengths))  82.7 us
    dot_general x4, matrix products, attend_backward(): jnp.einsum('hqk,khe->qhe', d_scores, split_heads(k_rows), preferred_eleme...  81 us
    dot_general x4, matrix products, attend_backward(): jnp.einsum('qhe,khe->hqk', split_heads(d_rows), split_heads(v_rows), pref...  79.2 us
    all_gather x1, waiting for transfers between devices, shards(): lax.all_gather(keys_own, 'seq', axis=1, tiled=True)  70 us
    reduce_scatter x1, waiting for transfers between devices, shards(): lax.psum_scatter(grad_qkv.astype(jnp.bfloat16), 'batch', scatter_dimensio...  68.8 us
    dynamic_slice x32, local copies, waits for them, and re-layouts, shards(): lax.map(forward_one, (query, keys_all, values_all, lengths))  68.2 us
    psum x1, waiting for transfers between devices, shards(): lax.psum(shares[2].astype(jnp.bfloat16), 'seq').astype(jnp.float32)  63.3 us
  transfers between devices with their start and end apart: 12, of which 5 were waited for; matrix products, arithmetic and copies ran while one was open for 67% of the time, Pallas kernels for 0%

profile of v1, /device:TPU:0, one launch (start us, length us, event | category | flops | bytes accessed | tf_op | source)
XLA Modules:
  0.0 1321.5 jit_solution(17202872314901679159)
XLA Ops:
  23.6 13.4 %constant_dynamic-update-slice_fusion.1 = f32[4,258,2304]{2,0,1:T(4,128)} fusion(f32[4,258,2304]{2,0,1:T(4,128)} %constant_dynamic-update-slice_fusion.2, f32[4,256,2304]{2,1,0:T(8,128)} %copy-done.2), kind=kLoop, calls=%fused_computation.113 | loop fusion | bytes 18874368 | tf_op jit(solution)/shard_map/concatenate | solution.py:120
  37.0 17.5 %add_convert_fusion.1 = bf16[4,256,2304]{2,0,1:T(4,128)(2,1)S(1)} fusion(f32[4,258,2304]{2,0,1:T(4,128)} %constant_dynamic-update-slice_fusion.1, f32[2304]{0:T(1024)S(1)} %get-tuple-element.212, f32[2304]{0:T(1024)} %get-tuple-element.213, f32[2304]{0:T(1024)} %get-tuple-element.211, f32[4,256,2304]{2,1,0:T(8,128)} %copy-done.2), kind=kLoop, calls=%fused_computation.52 | loop fusion | flops 14155776 | bytes 33057792 | tf_op jit(solution)/shard_map/convert_element_type | solution.py:125
  64.8 70.0 %all-gather.9.cloned.1.call-done = bf16[4,2048,768]{2,0,1:T(4,128)(2,1)} async-done(((bf16[4,256,768]{2,0,1:T(4,128)(2,1)}), bf16[4,2048,768]{2,0,1:T(4,128)(2,1)}) %all-gather.9.cloned.1.call-update) | async-done | bytes 12582928 | tf_op jit(solution)/shard_map/all_gather | solution.py:130
  134.8 20.3 %copy.104 = bf16[4,2048,768]{1,2,0:T(8,128)(2,1)} copy(bf16[4,2048,768]{2,0,1:T(4,128)(2,1)} %all-gather.9.cloned.1.call-done) | data formatting | bytes 25165824 | tf_op jit(solution)/shard_map/while | solution.py:137
  155.1 53.7 %all-gather.7.cloned.1.call-done = bf16[4,2048,768]{2,0,1:T(4,128)(2,1)} async-done(((bf16[4,256,768]{2,0,1:T(4,128)(2,1)}), bf16[4,2048,768]{2,0,1:T(4,128)(2,1)}) %all-gather.7.cloned.1.call-update) | async-done | bytes 12582928 | tf_op jit(solution)/shard_map/all_gather | solution.py:131
  208.9 20.3 %copy.102 = bf16[4,2048,768]{1,2,0:T(8,128)(2,1)} copy(bf16[4,2048,768]{2,0,1:T(4,128)(2,1)} %all-gather.7.cloned.1.call-done) | data formatting | bytes 25165824 | tf_op jit(solution)/shard_map/while | solution.py:137
  229.7 170.4 %while.24 = (s32[]{:T(128)}, bf16[4,256,768]{1,2,0:T(8,128)(2,1)}, f32[4,12,256]{2,1,0:T(8,128)}, bf16[4,2048,768]{1,2,0:T(8,128)(2,1)}, s32[]{:T(128)}, /*index...) while((s32[]{:T(128)}, bf16[4,256,768]{1,2,0:T(8,128)(2,1)}, ...), condition=%wide.region_4.5_spmd, body=%wide.region_1.4_spmd.sunk | while | flops 1687158016 | bytes 98936960 | solution.py:137
  236.5 12.3 fusion.108
  248.8 11.6 fusion.109
  260.4 12.0 fusion.110
  280.6 10.6 fusion.108
  291.2 11.5 fusion.109
  302.8 11.8 fusion.110
  322.7 10.6 fusion.108
  333.4 11.5 fusion.109
  344.9 11.8 fusion.110
  364.8 10.6 fusion.108
  375.5 11.5 fusion.109
  387.0 11.8 fusion.110
  430.8 10.5 multiply_reduce_fusion.6
  464.1 10.4 bitcast_convert_fusion
  475.2 350.5 %while.25 = (s32[]{:T(128)}, f32[4,256,768]{2,0,1:T(4,128)}, f32[4,12,256]{2,1,0:T(8,128)}, bf16[4,2048,768]{1,2,0:T(8,128)(2,1)}, s32[]{:T(128)}, /*index=5*/s3...) while((s32[]{:T(128)}, f32[4,256,768]{2,0,1:T(4,128)}, ...), condition=%wide.region_9.10_spmd, body=%wide.region_7.9_spmd.sunk | while | flops 2486369536 | bytes 169195712 | solution.py:180
  492.8 10.3 fusion.116
  503.1 19.8 %multiply_reduce_fusion.14 = (f32[12,256]{1,0:T(8,128)}, f32[12,256,2048]{2,1,0:T(8,128)}) fusion(f32[12,256,2048]{2,1,0:T(8,128)} %fusion.116, f32[12,256]{1,0:T(8,128)S(1)} %dynamic-slice_bitcast_fusion.2, pred[256,2048]{1,0:T(8,128)(4,1)} %fusion.117, bf16[256,12,64]{0,2,1:T(8,128)(2,1)} %bitcast.150, bf16[2048,12,64]{0,2,1:T(8,128)(2,1)} %bitcast.143), kind=kOutput, calls=%fused_computation.18.clone.1 | convolution fusion | flops 836760576 | bytes 54419456 | tf_op jit(solution)/shard_map/while/body/eval_jaxpr/qhe,khe->hqk/dot_general | solution.py:76
  522.9 20.4 %fusion.118 = f32[12,64,256]{2,1,0:T(8,128)} fusion(bf16[2048,12,64]{0,2,1:T(8,128)(2,1)} %bitcast.141, f32[12,256,2048]{2,1,0:T(8,128)} %get-tuple-element.412, f32[12,256,2048]{2,1,0:T(8,128)} %fusion.116, f32[12,256]{1,0:T(8,128)} %get-tuple-element.413, f32[12,256]{1,0:T(8,128)S(1)} %dynamic-slice_bitcast_fusion.2, pred[256,2048]{1,0:T(8,128)(4,1)} %fusion.117), kind=kOutput, calls=%fused_computation.24.clone.1 | convolution fusion | flops 843251712 | bytes 54812672 | tf_op jit(solution)/shard_map/while/body/eval_jaxpr/hqk,khe->qhe/dot_general | solution.py:83
  547.8 15.6 %dynamic_update_slice.24 = f32[4,256,768]{2,0,1:T(4,128)} dynamic-update-slice(f32[4,256,768]{2,0,1:T(4,128)} %get-tuple-element.454, f32[1,256,768]{2,0,1:T(1,128)} %copy.160, s32[]{:T(128)S(6)} %copy.178, s32[]{:T(128)} %constant.67.clone.1..sunk, s32[]{:T(128)} %constant.67.clone.1..sunk) | dynamic-update-slice | bytes 1572868 | tf_op jit(solution)/shard_map/while/body/jit(dynamic_update_index_in_dim)/dynamic_update_slice | solution.py:137
  591.0 19.8 %multiply_reduce_fusion.14 = (f32[12,256]{1,0:T(8,128)}, f32[12,256,2048]{2,1,0:T(8,128)}) fusion(f32[12,256,2048]{2,1,0:T(8,128)} %fusion.116, f32[12,256]{1,0:T(8,128)S(1)} %dynamic-slice_bitcast_fusion.2, pred[256,2048]{1,0:T(8,128)(4,1)} %fusion.117, bf16[256,12,64]{0,2,1:T(8,128)(2,1)} %bitcast.150, bf16[2048,12,64]{0,2,1:T(8,128)(2,1)} %bitcast.143), kind=kOutput, calls=%fused_computation.18.clone.1 | convolution fusion | flops 836760576 | bytes 54419456 | tf_op jit(solution)/shard_map/while/body/eval_jaxpr/qhe,khe->hqk/dot_general | solution.py:76
  610.8 20.3 %fusion.118 = f32[12,64,256]{2,1,0:T(8,128)} fusion(bf16[2048,12,64]{0,2,1:T(8,128)(2,1)} %bitcast.141, f32[12,256,2048]{2,1,0:T(8,128)} %get-tuple-element.412, f32[12,256,2048]{2,1,0:T(8,128)} %fusion.116, f32[12,256]{1,0:T(8,128)} %get-tuple-element.413, f32[12,256]{1,0:T(8,128)S(1)} %dynamic-slice_bitcast_fusion.2, pred[256,2048]{1,0:T(8,128)(4,1)} %fusion.117), kind=kOutput, calls=%fused_computation.24.clone.1 | convolution fusion | flops 843251712 | bytes 54812672 | tf_op jit(solution)/shard_map/while/body/eval_jaxpr/hqk,khe->qhe/dot_general | solution.py:83
  635.5 15.5 %dynamic_update_slice.24 = f32[4,256,768]{2,0,1:T(4,128)} dynamic-update-slice(f32[4,256,768]{2,0,1:T(4,128)} %get-tuple-element.454, f32[1,256,768]{2,0,1:T(1,128)} %copy.160, s32[]{:T(128)S(6)} %copy.178, s32[]{:T(128)} %constant.67.clone.1..sunk, s32[]{:T(128)} %constant.67.clone.1..sunk) | dynamic-update-slice | bytes 1572868 | tf_op jit(solution)/shard_map/while/body/jit(dynamic_update_index_in_dim)/dynamic_update_slice | solution.py:137
  678.5 19.8 %multiply_reduce_fusion.14 = (f32[12,256]{1,0:T(8,128)}, f32[12,256,2048]{2,1,0:T(8,128)}) fusion(f32[12,256,2048]{2,1,0:T(8,128)} %fusion.116, f32[12,256]{1,0:T(8,128)S(1)} %dynamic-slice_bitcast_fusion.2, pred[256,2048]{1,0:T(8,128)(4,1)} %fusion.117, bf16[256,12,64]{0,2,1:T(8,128)(2,1)} %bitcast.150, bf16[2048,12,64]{0,2,1:T(8,128)(2,1)} %bitcast.143), kind=kOutput, calls=%fused_computation.18.clone.1 | convolution fusion | flops 836760576 | bytes 54419456 | tf_op jit(solution)/shard_map/while/body/eval_jaxpr/qhe,khe->hqk/dot_general | solution.py:76
  698.3 20.1 %fusion.118 = f32[12,64,256]{2,1,0:T(8,128)} fusion(bf16[2048,12,64]{0,2,1:T(8,128)(2,1)} %bitcast.141, f32[12,256,2048]{2,1,0:T(8,128)} %get-tuple-element.412, f32[12,256,2048]{2,1,0:T(8,128)} %fusion.116, f32[12,256]{1,0:T(8,128)} %get-tuple-element.413, f32[12,256]{1,0:T(8,128)S(1)} %dynamic-slice_bitcast_fusion.2, pred[256,2048]{1,0:T(8,128)(4,1)} %fusion.117), kind=kOutput, calls=%fused_computation.24.clone.1 | convolution fusion | flops 843251712 | bytes 54812672 | tf_op jit(solution)/shard_map/while/body/eval_jaxpr/hqk,khe->qhe/dot_general | solution.py:83
  722.8 15.5 %dynamic_update_slice.24 = f32[4,256,768]{2,0,1:T(4,128)} dynamic-update-slice(f32[4,256,768]{2,0,1:T(4,128)} %get-tuple-element.454, f32[1,256,768]{2,0,1:T(1,128)} %copy.160, s32[]{:T(128)S(6)} %copy.178, s32[]{:T(128)} %constant.67.clone.1..sunk, s32[]{:T(128)} %constant.67.clone.1..sunk) | dynamic-update-slice | bytes 1572868 | tf_op jit(solution)/shard_map/while/body/jit(dynamic_update_index_in_dim)/dynamic_update_slice | solution.py:137
  765.8 19.8 %multiply_reduce_fusion.14 = (f32[12,256]{1,0:T(8,128)}, f32[12,256,2048]{2,1,0:T(8,128)}) fusion(f32[12,256,2048]{2,1,0:T(8,128)} %fusion.116, f32[12,256]{1,0:T(8,128)S(1)} %dynamic-slice_bitcast_fusion.2, pred[256,2048]{1,0:T(8,128)(4,1)} %fusion.117, bf16[256,12,64]{0,2,1:T(8,128)(2,1)} %bitcast.150, bf16[2048,12,64]{0,2,1:T(8,128)(2,1)} %bitcast.143), kind=kOutput, calls=%fused_computation.18.clone.1 | convolution fusion | flops 836760576 | bytes 54419456 | tf_op jit(solution)/shard_map/while/body/eval_jaxpr/qhe,khe->hqk/dot_general | solution.py:76
  785.6 20.1 %fusion.118 = f32[12,64,256]{2,1,0:T(8,128)} fusion(bf16[2048,12,64]{0,2,1:T(8,128)(2,1)} %bitcast.141, f32[12,256,2048]{2,1,0:T(8,128)} %get-tuple-element.412, f32[12,256,2048]{2,1,0:T(8,128)} %fusion.116, f32[12,256]{1,0:T(8,128)} %get-tuple-element.413, f32[12,256]{1,0:T(8,128)S(1)} %dynamic-slice_bitcast_fusion.2, pred[256,2048]{1,0:T(8,128)(4,1)} %fusion.117), kind=kOutput, calls=%fused_computation.24.clone.1 | convolution fusion | flops 843251712 | bytes 54812672 | tf_op jit(solution)/shard_map/while/body/eval_jaxpr/hqk,khe->qhe/dot_general | solution.py:83
  810.1 15.5 %dynamic_update_slice.24 = f32[4,256,768]{2,0,1:T(4,128)} dynamic-update-slice(f32[4,256,768]{2,0,1:T(4,128)} %get-tuple-element.454, f32[1,256,768]{2,0,1:T(1,128)} %copy.160, s32[]{:T(128)S(6)} %copy.178, s32[]{:T(128)} %constant.67.clone.1..sunk, s32[]{:T(128)} %constant.67.clone.1..sunk) | dynamic-update-slice | bytes 1572868 | tf_op jit(solution)/shard_map/while/body/jit(dynamic_update_index_in_dim)/dynamic_update_slice | solution.py:137
  825.6 10.9 all_gather.27
  836.5 11.3 all_gather.29
  857.8 20.1 %copy.110 = bf16[4,2048,768]{1,2,0:T(8,128)(2,1)} copy(bf16[4,2048,768]{2,0,1:T(4,128)(2,1)} %all-gather.11.cloned.1.call-done) | data formatting | bytes 25165824 | tf_op jit(solution)/shard_map/all_gather | solution.py:188
  877.9 39.7 %fusion.62 = f32[4,12,2048,256]{3,2,1,0:T(8,128)} fusion(bf16[4,2048,12,64]{1,3,2,0:T(8,128)(2,1)} %bitcast.148, bf16[4,256,12,64]{1,3,2,0:T(8,128)(2,1)} %bitcast.154), kind=kOutput, calls=%fused_computation.137 | convolution fusion | flops 3221225472 | bytes 114819072 | tf_op jit(solution)/shard_map/vmap(qhe,khe->hqk)/dot_general | solution.py:46
  917.6 16.7 %copy.112 = bf16[4,2048,768]{1,2,0:T(8,128)(2,1)} copy(bf16[4,2048,768]{2,1,0:T(8,128)(2,1)} %all-gather.13.cloned.1.call-done) | data formatting | bytes 25165824 | tf_op jit(solution)/shard_map/all_gather | solution.py:189
  934.3 38.9 %fusion.13 = f32[4,12,64,256]{3,2,1,0:T(8,128)} fusion(bf16[4,2048,12,64]{1,3,2,0:T(8,128)(2,1)} %bitcast.151, f32[4,12,2048,256]{3,2,1,0:T(8,128)} %fusion.62, f32[4,12,2048]{2,1,0:T(8,128)} %all_gather.27, pred[4,2048,256]{2,1,0:T(8,128)(4,1)} %broadcast_and_fusion), kind=kOutput, calls=%fused_computation.38 | convolution fusion | flops 3321888768 | bytes 118882304 | tf_op jit(solution)/shard_map/vmap(hqk,qhe->khe)/dot_general | solution.py:207
  978.2 51.0 %fusion.42 = f32[4,12,64,256]{3,2,1,0:T(8,128)} fusion(bf16[4,2048,12,64]{1,3,2,0:T(8,128)(2,1)} %bitcast.149, f32[4,12,2048,256]{3,2,1,0:T(8,128)} %fusion.62, f32[4,12,2048]{2,1,0:T(8,128)} %all_gather.29, f32[4,12,2048]{2,1,0:T(8,128)} %all_gather.27, pred[4,2048,256]{2,1,0:T(8,128)(4,1)} %broadcast_and_fusion, bf16[4,2048,12,64]{1,3,2,0:T(8,128)(2,1)} %bitcast.152, ...), kind=kOutput, calls=%fused_computation.94 | convolution fusion | flops 6594232320 | bytes 133431296 | tf_op jit(solution)/shard_map/vmap(hqk,qhe->khe)/dot_general | solution.py:202
  1034.2 20.5 %multiply_reduce_fusion.2 = (f32[2304]{0:T(1024)}, f32[2304]{0:T(1024)}, f32[2304]{0:T(1024)S(1)}, f32[4,256,2304]{2,0,1:T(4,128)S(1)}) fusion(f32[4,258,2304]{2,0,1:T(4,128)} %constant_dynamic-update-slice_fusion.1, f32[4,256,768]{2,0,1:T(4,128)} %copy.116, f32[4,256,768]{2,0,1:T(4,128)} %copy.115, f32[4,256,768]{2,0,1:T(4,128)} %get-tuple-element.108, ...), kind=kLoop, calls=%fused_computation.49 | loop fusion | flops 18867456 | bytes 47213568 | tf_op jit(solution)/shard_map/reduce_sum | solution.py:236
  1075.7 68.8 %reduce-scatter.5.cloned.1.call-done = bf16[192,2304]{1,0:T(8,128)(2,1)} async-done(((bf16[768,2304]{1,0:T(8,128)(2,1)}), bf16[192,2304]{1,0:T(8,128)(2,1)}) %reduce-scatter.5.cloned.1.call-update) | async-done | bytes 884752 | tf_op jit(solution)/shard_map/reduce_scatter | solution.py:250
  1150.9 63.3 %all-reduce.10.cloned.1.call-done = (bf16[192,768]{1,0:T(8,128)(2,1)}, bf16[192,3072]{1,0:T(8,128)(2,1)}, bf16[768,768]{1,0:T(8,128)(2,1)}) async-done(((bf16[192,768]{1,0:T(8,128)(2,1)}, bf16[192,3072]{1,0:T(8,128)(2,1)}, bf16[768,768]{1,0:T(8,128)(2,1)}), (bf16[192,768]{1,0:T(8,128)(2,1)}, bf16[192,3072]{1,0:T(8,128)(2,1)}, bf16[768,768]{1,0:T(8,128)(2,1)})) %all-reduce.10.cloned.1.call-update) | async-done | bytes 2654224 | tf_op jit(solution)/shard_map/psum | solution.py:269
  1221.4 40.7 %all-reduce.4 = (f32[3,2304]{1,0:T(4,128)}, f32[4]{0:T(128)S(1)}) all-reduce(f32[3,2304]{1,0:T(4,128)} %pad_maximum_fusion.2, f32[4]{0:T(128)} %pad_maximum_fusion.3), channel_id=1, replica_groups=mesh['seq'=8,'batch'=4] {'seq','batch'}, use_global_device_ids=true, to_apply=%region_19.20 | all-reduce | flops 6916 | bytes 55328 | tf_op jit(solution)/shard_map/psum | solution.py:274
  1273.1 11.3 all-reduce.7
  1286.4 12.5 all-reduce.5
  (249 shorter events, 313.3 us)
Async XLA Ops:
  7.2 3.5 copy-start
  7.2 127.6 %all-gather.9.cloned.1.call-start = ((), (), s32[]{:S(2)}) async-start(), calls=%async_computation.5 | async-start | bytes 14155776 | tf_op jit(solution)/shard_map/all_gather | solution.py:130
  8.1 8.0 copy-start.24
  10.7 5.4 copy-start.21
  10.7 11.6 copy-start.17
  16.1 3.6 copy-start.2
  19.7 3.3 collective-permute-start
  22.9 14.0 %copy-start.9 = (f32[2304]{0:T(1024)}, f32[2304]{0:T(1024)S(1)}, u32[]{:S(2)}) copy-start(f32[2304]{0:T(1024)S(1)} %get-tuple-element.212) | copy-start | bytes 27652
  54.5 3.7 copy-start.31
  54.5 4.9 copy-start.30
  57.4 151.4 %all-gather.7.cloned.1.call-start = ((), (), s32[]{:S(2)}) async-start(), calls=%async_computation.4 | async-start | bytes 14155776 | tf_op jit(solution)/shard_map/all_gather | solution.py:131
  58.2 799.6 %all-gather.11.cloned.1.call-start = ((), (), s32[]{:S(2)}) async-start(), calls=%async_computation.6 | async-start | bytes 14155776 | tf_op jit(solution)/shard_map/all_gather | solution.py:188
  64.5 853.1 %all-gather.13.cloned.1.call-start = ((), (), s32[]{:S(2)}) async-start(), calls=%async_computation.7 | async-start | bytes 14155776 | tf_op jit(solution)/shard_map/all_gather | solution.py:189
  400.2 5.1 copy-start.19
  400.2 5.1 copy-start.33
  400.2 13.6 %slice-start = ((s8[4718592]{0:T(1024)(128)(4,1)}), s8[4194304]{0:T(1024)(128)(4,1)S(1)}, s32[]{:S(2)}) async-start(s8[4718592]{0:T(1024)(128)(4,1)} %bitcast.159), calls=%async_computation.14 | async-start | bytes 8388608
  405.2 36.1 %copy-start.6 = (f32[4,256,768]{2,1,0:T(8,128)}, f32[4,256,768]{2,1,0:T(8,128)S(1)}, u32[]{:S(2)}) copy-start(f32[4,256,768]{2,1,0:T(8,128)S(1)} %get-tuple-element.266) | copy-start | bytes 9437188
  405.2 36.1 %copy-start.18 = (f32[4,256]{1,0:T(4,128)}, f32[4,256]{1,0:T(4,128)S(1)}, u32[]{:S(2)}) copy-start(f32[4,256]{1,0:T(4,128)S(1)} %get-tuple-element.286) | copy-start | bytes 12292
  405.3 8.5 copy-start.7
  405.3 8.5 copy-start.15
  405.3 8.5 slice-start.1
  441.3 2.8 copy-start.34
  444.1 2.7 copy-start.29
  446.8 628.2 %reduce-scatter.7.cloned.1.call-start = ((), (), s32[]{:S(2)}) async-start(), calls=%async_computation.9 | async-start | bytes 1474560 | tf_op jit(solution)/shard_map/reduce_scatter | solution.py:253
  448.0 5.1 copy-start.27
  452.8 622.2 %reduce-scatter.11.cloned.1.call-start = ((), (), s32[]{:S(2)}) async-start(), calls=%async_computation.11 | async-start | bytes 5898240 | tf_op jit(solution)/shard_map/reduce_scatter | solution.py:262
  474.5 600.5 %reduce-scatter.9.cloned.1.call-start = ((), (), s32[]{:S(2)}) async-start(), calls=%async_computation.10 | async-start | bytes 5898240 | tf_op jit(solution)/shard_map/reduce_scatter | solution.py:259
  491.0 1.8 copy-start.1
  579.1 1.8 copy-start.1
  857.7 286.8 %reduce-scatter.5.cloned.1.call-start = ((), (), s32[]{:S(2)}) async-start(), calls=%async_computation.8 | async-start | bytes 4423680 | tf_op jit(solution)/shard_map/reduce_scatter | solution.py:250
  1034.2 20.6 %copy-start.10 = (f32[2304]{0:T(1024)S(1)}, f32[2304]{0:T(1024)}, u32[]{:S(2)}) copy-start(f32[2304]{0:T(1024)} %copy-done.9) | copy-start | bytes 27652
  1034.2 20.6 %copy-start.11 = (f32[2304]{0:T(1024)S(1)}, f32[2304]{0:T(1024)}, u32[]{:S(2)}) copy-start(f32[2304]{0:T(1024)} %get-tuple-element.213) | copy-start | bytes 27652
  1034.2 23.9 %copy-start.12 = (f32[2304]{0:T(1024)S(1)}, f32[2304]{0:T(1024)}, u32[]{:S(2)}) copy-start(f32[2304]{0:T(1024)} %get-tuple-element.211) | copy-start | bytes 27652
  1054.8 14.5 %copy-start.4 = (bf16[4,256,768]{2,1,0:T(8,128)(2,1)S(1)}, bf16[4,256,768]{2,1,0:T(8,128)(2,1)}, u32[]{:S(2)}) copy-start(bf16[4,256,768]{2,1,0:T(8,128)(2,1)} %param.15) | copy-start | bytes 4718596
  1054.8 14.5 %copy-start.22 = (f32[4,256]{1,0:T(4,128)S(1)}, f32[4,256]{1,0:T(4,128)}, u32[]{:S(2)}) copy-start(f32[4,256]{1,0:T(4,128)} %copy-done.21) | copy-start | bytes 12292
  1054.8 14.5 %copy-start.25 = (f32[768]{0:T(1024)S(1)}, f32[768]{0:T(1024)}, u32[]{:S(2)}) copy-start(f32[768]{0:T(1024)} %copy-done.24) | copy-start | bytes 9220
  1054.8 3.2 collective-permute-start.1
  1067.1 2.2 copy-start.5
  1074.9 71.6 %copy-start.16 = (f32[4,256]{1,0:T(4,128)S(1)}, f32[4,256]{1,0:T(4,128)}, u32[]{:S(2)}) copy-start(f32[4,256]{1,0:T(4,128)} %get-tuple-element.263) | copy-start | bytes 12292
  1074.9 139.3 %all-reduce.10.cloned.1.call-start = ((), (), s32[]{:S(2)}) async-start(), calls=%async_computation.13 | async-start | bytes 5308416 | tf_op jit(solution)/shard_map/psum | solution.py:269
  1075.6 231.2 %all-gather.15.cloned.1.call-start = ((), (), s32[]{:S(2)}) async-start(), calls=%async_computation.12 | async-start | bytes 7962624 | tf_op jit(solution)/shard_map/all_gather | solution.py:12
  1214.2 4.9 copy-start.8
  1216.1 4.6 copy-start.14
  1216.1 4.6 copy-start.13
  1216.1 47.7 %copy-start.23 = (f32[4,256]{1,0:T(4,128)S(1)}, f32[4,256]{1,0:T(4,128)}, u32[]{:S(2)}) copy-start(f32[4,256]{1,0:T(4,128)} %copy-done.21) | copy-start | bytes 12292
  1263.8 9.3 copy-start.32
  1263.8 38.1 %copy-start.20 = (f32[4,256]{1,0:T(4,128)S(1)}, f32[4,256]{1,0:T(4,128)}, u32[]{:S(2)}) copy-start(f32[4,256]{1,0:T(4,128)} %get-tuple-element.283) | copy-start | bytes 12292
  1263.8 38.1 %copy-start.26 = (f32[768]{0:T(1024)S(1)}, f32[768]{0:T(1024)}, u32[]{:S(2)}) copy-start(f32[768]{0:T(1024)} %copy-done.24) | copy-start | bytes 9220
  (4 other events, 5.7 us)
Sparse Core Ops, SparseCore 0:
  57.5 77.2 all-gather.8
  136.7 72.1 all-gather.6
  210.8 72.1 all-gather.10
  446.9 72.2 all-gather.12
  521.3 29.1 reduce-scatter.6
  552.7 83.9 reduce-scatter.10
  857.8 85.3 reduce-scatter.8
  1075.0 69.4 reduce-scatter.4
  1148.1 66.0 all-reduce.9
  1216.1 49.7 all-gather.14
